TPU v7x, 256 devices: a whole 4x4x8 slice. The times are simulated.
256 devices in a mesh: past: 32 (over y, x, core), second: 8 (over z).
Axes of the slice: x: 4, y: 4, z: 8, core: 2. Of those that a mesh axis runs over, the one named last changes fastest.
Arguments:
- g_hist: bfloat16 [65536, 8192], P('past', 'second'), may hold values from -6 to 6
- sigma_hist: bfloat16 [1024, 65536], P(None, 'past'), may hold values from -0.046875 to 0.046875
- volterra: bfloat16 [2, 512, 1024], replicated, may hold values from -0.1875 to 0.1875
- sigma_edge: bfloat16 [512, 8192], P(None, 'second'), may hold values from -6 to 6
- coupling: float32 [32, 8192], P(None, 'second'), may hold values from 0.3 to 3
Outputs:
- g_new: bfloat16 [1024, 8192], P(None, 'second')
- sigma_new: bfloat16 [1024, 8192], P(None, 'second')
All inputs are finite; a program needn't handle non-finite values.
Results may differ from a plain program's by a relative error of at most 0.0059.
Values may be sent and summed in bfloat16 or wider, within the bound.
A program may use at most 64 MiB of HBM per device.

v0:
```python
import jax
import jax.numpy as jnp
from jax import lax
from jax.sharding import PartitionSpec as P

N = 32
BLK = 16
NB = 2


def per_device(g_hist, sigma_hist, volterra, sigma_edge, coupling):
    rows = BLK * N
    columns = g_hist.shape[1]
    count_all = rows * columns * lax.axis_size("second")
    prev = sigma_edge
    g_blocks = []
    s_blocks = []
    for block in range(NB):
        sig_rows = sigma_hist[block * rows : (block + 1) * rows, :]
        w_memory = volterra[block][:, :rows]
        w_sigma = volterra[block][:, rows:]
        start_value = jnp.dot(w_sigma, prev, preferred_element_type=jnp.float32)
        mine = lax.psum_scatter(
            jnp.dot(sig_rows, g_hist, preferred_element_type=jnp.float32),
            "past",
            scatter_dimension=0,
            tiled=True,
        ).astype(jnp.bfloat16)
        gnew = start_value + jnp.dot(
            w_memory,
            lax.all_gather(mine, "past", axis=0, tiled=True),
            preferred_element_type=jnp.float32,
        )
        cubic = gnew.reshape(BLK, N, columns) ** 3 * coupling[None]
        local_sq = jnp.sum(cubic * cubic)
        total_sq = lax.psum(local_sq, "second")
        meansq = total_sq / count_all
        sigma = (cubic / jnp.sqrt(meansq + 1e-06)).reshape(rows, columns).astype(jnp.bfloat16)
        g_blocks.append(gnew.astype(jnp.bfloat16))
        s_blocks.append(sigma)
        prev = sigma
    return (jnp.concatenate(g_blocks, axis=0), jnp.concatenate(s_blocks, axis=0))


def solution(mesh):
    return jax.shard_map(
        per_device,
        mesh=mesh,
        in_specs=(P("past", "second"), P(None, "past"), P(), P(None, "second"), P(None, "second")),
        out_specs=(P(None, "second"), P(None, "second")),
        check_vma=False,
    )
```

profile of v0, /device:TPU:2, one launch (start us, length us, event | category | flops | bytes accessed | tf_op | source)
XLA Modules:
  0.0 328.4 jit_solution(678575552743775766)
XLA Ops:
  7.2 0.0 reduce-scatter.3.cloned.1.call-start
  7.2 6.5 %fusion.2 = f32[512,1024]{1,0:T(8,128)} fusion(bf16[2048,1024]{1,0:T(8,128)(2,1)} %param.5, bf16[1024,2048]{1,0:T(8,128)(2,1)} %param.6), kind=kOutput, calls=%fused_computation.14 | convolution fusion | flops 2147483648 | bytes 8388608 | tf_op jit(solution)/shard_map/dot_general | solution.py:24
  13.8 0.0 reduce-scatter.3.cloned.1.call-update
  13.8 0.0 reduce-scatter.5.cloned.1.call-start
  13.8 6.5 %fusion = f32[512,1024]{1,0:T(8,128)} fusion(bf16[2048,1024]{1,0:T(8,128)(2,1)} %param.5, bf16[1024,2048]{1,0:T(8,128)(2,1)} %param.6), kind=kOutput, calls=%fused_computation.10 | convolution fusion | flops 2147483648 | bytes 8388608 | tf_op jit(solution)/shard_map/dot_general | solution.py:24
  20.4 0.0 all-gather.3.cloned.1.call-start
  20.4 82.8 %reduce-scatter.3.cloned.1.call-done = f32[16,1024]{1,0:T(8,128)} async-done(((f32[512,1024]{1,0:T(8,128)}), f32[16,1024]{1,0:T(8,128)}) %reduce-scatter.3.cloned.1.call-update) | async-done | bytes 65552 | tf_op jit(solution)/shard_map/reduce_scatter | solution.py:23
  103.2 1.5 convert_element_type.18
  104.6 0.0 all-gather.3.cloned.1.call-update
  104.7 0.0 all-gather.5.cloned.1.call-start
  104.7 88.8 %reduce-scatter.5.cloned.1.call-done = f32[16,1024]{1,0:T(8,128)} async-done(((f32[512,1024]{1,0:T(8,128)}), f32[16,1024]{1,0:T(8,128)}) %reduce-scatter.5.cloned.1.call-update) | async-done | bytes 65552 | tf_op jit(solution)/shard_map/reduce_scatter | solution.py:23
  193.6 1.4 convert_element_type.21
  195.0 0.0 all-gather.5.cloned.1.call-update
  195.0 1.1 slice_bitcast_fusion
  196.2 1.0 copy-done.4
  197.2 0.7 fusion.8
  197.9 45.8 %all-gather.3.cloned.1.call-done = bf16[512,1024]{1,0:T(8,128)(2,1)} async-done(((bf16[16,1024]{1,0:T(8,128)(2,1)}), bf16[512,1024]{1,0:T(8,128)(2,1)}) %all-gather.3.cloned.1.call-update) | async-done | bytes 1048592 | tf_op jit(solution)/shard_map/all_gather | solution.py:31
  243.7 4.1 %multiply_reduce_fusion.1 = (f32[]{:T(128)}, f32[512,1024]{1,0:T(8,128)}) fusion(f32[32,1024]{1,0:T(8,128)S(1)} %copy-done.7, f32[512,1024]{1,0:T(8,128)S(1)} %fusion.8, bf16[512,1024]{1,0:T(8,128)(2,1)} %all-gather.3.cloned.1.call-done, bf16[512,1024]{1,0:T(8,128)(2,1)} %copy-done.4), kind=kOutput, calls=%fused_computation.13 | convolution fusion | flops 540016640 | bytes 5898244 | tf_op jit(solution)/shard_map/dot_general | solution.py:29
  247.8 18.1 %psum.14 = f32[]{:T(128)} all-reduce(f32[]{:T(128)} %get-tuple-element.6), channel_id=1, replica_groups=mesh['past'=32,'second'=8] {'second'}, use_global_device_ids=true, to_apply=%region_2.0 | all-reduce | flops 1 | bytes 8 | tf_op jit(solution)/shard_map/psum | solution.py:36
  266.6 3.8 %fusion.10 = (bf16[512,1024]{1,0:T(8,128)(2,1)}, bf16[512,1024]{1,0:T(8,128)(2,1)S(1)}) fusion(f32[512,1024]{1,0:T(8,128)} %get-tuple-element.7, f32[]{:T(128)S(6)} %sqrt.6, f32[32,1024]{1,0:T(8,128)S(1)} %copy-done.7), kind=kLoop, calls=%fused_computation.25 | loop fusion | flops 3145728 | bytes 4325380 | tf_op jit(solution)/shard_map/convert_element_type | solution.py:39
  270.4 1.0 copy-done.1
  271.4 2.0 fusion.5
  273.4 19.7 %all-gather.5.cloned.1.call-done = bf16[512,1024]{1,0:T(8,128)(2,1)} async-done(((bf16[16,1024]{1,0:T(8,128)(2,1)}), bf16[512,1024]{1,0:T(8,128)(2,1)}) %all-gather.5.cloned.1.call-update) | async-done | bytes 1048592 | tf_op jit(solution)/shard_map/all_gather | solution.py:31
  293.1 3.8 %bitcast_convert_fusion = (bf16[512,1024]{1,0:T(8,128)(2,1)}, f32[1024,512]{0,1:T(8,128)S(1)}) fusion(f32[1024,512]{0,1:T(8,128)} %fusion.5, bf16[512,1024]{1,0:T(8,128)(2,1)} %all-gather.5.cloned.1.call-done, bf16[512,1024]{1,0:T(8,128)(2,1)} %get-tuple-element.4), kind=kOutput, calls=%fused_computation.6 | convolution fusion | flops 537919488 | bytes 6815744 | tf_op jit(solution)/shard_map/dot_general | solution.py:29
  296.9 1.1 multiply_reduce_fusion
  298.1 18.1 %psum.15 = f32[]{:T(128)} all-reduce(f32[]{:T(128)} %multiply_reduce_fusion), channel_id=1, replica_groups=mesh['past'=32,'second'=8] {'second'}, use_global_device_ids=true, to_apply=%region_5.0 | all-reduce | flops 1 | bytes 8 | tf_op jit(solution)/shard_map/psum | solution.py:36
  316.8 0.3 divide_convert_fusion
  317.2 0.9 copy-done.2
  318.1 1.5 pad_maximum_fusion.1
  319.6 0.0 copy-done.3
  319.6 0.8 copy-done.6
  320.4 1.5 pad_maximum_fusion
  (14 shorter events, 0.0 us)
Async XLA Ops:
  7.2 190.0 %copy-start = (bf16[512,1024]{1,0:T(8,128)(2,1)S(1)}, bf16[512,1024]{1,0:T(8,128)(2,1)}, u32[]{:S(2)}) copy-start(bf16[512,1024]{1,0:T(8,128)(2,1)} %param.8) | copy-start | bytes 3145732
  7.2 96.0 %reduce-scatter.3.cloned.1.call-start = ((), (), s32[]{:S(2)}) async-start(), calls=%async_computation.2 | async-start | bytes 2162688 | tf_op jit(solution)/shard_map/reduce_scatter | solution.py:23
  13.8 179.8 %reduce-scatter.5.cloned.1.call-start = ((), (), s32[]{:S(2)}) async-start(), calls=%async_computation.4 | async-start | bytes 2162688 | tf_op jit(solution)/shard_map/reduce_scatter | solution.py:23
  20.3 174.7 %copy-start.8 = (bf16[2,512,1024]{2,1,0:T(8,128)(2,1)S(1)}, bf16[2,512,1024]{2,1,0:T(8,128)(2,1)}, u32[]{:S(2)}) copy-start(bf16[2,512,1024]{2,1,0:T(8,128)(2,1)} %param.7) | copy-start | bytes 6291460
  20.4 223.4 %all-gather.3.cloned.1.call-start = ((), (), s32[]{:S(2)}) async-start(), calls=%async_computation.3 | async-start | bytes 1081344 | tf_op jit(solution)/shard_map/all_gather | solution.py:31
  104.7 188.5 %all-gather.5.cloned.1.call-start = ((), (), s32[]{:S(2)}) async-start(), calls=%async_computation.5 | async-start | bytes 1081344 | tf_op jit(solution)/shard_map/all_gather | solution.py:31
  196.2 1.0 copy-start.4
  196.2 47.6 %copy-start.7 = (f32[32,1024]{1,0:T(8,128)S(1)}, f32[32,1024]{1,0:T(8,128)}, u32[]{:S(2)}) copy-start(f32[32,1024]{1,0:T(8,128)} %param.9) | copy-start | bytes 393220
  266.6 4.8 %copy-start.5 = (bf16[512,1024]{1,0:T(8,128)(2,1)S(1)}, bf16[512,1024]{1,0:T(8,128)(2,1)}, u32[]{:S(2)}) copy-start(bf16[512,1024]{1,0:T(8,128)(2,1)} %get-tuple-element.4) | copy-start | bytes 3145732
  270.4 1.0 copy-start.1
  316.8 1.2 copy-start.2
  318.1 1.5 copy-start.3
  318.1 2.3 copy-start.6
Sparse Core Ops, SparseCore 0:
  13.9 89.2 reduce-scatter.2
  107.6 85.9 reduce-scatter.4
  196.7 46.9 all-gather.2
  246.1 46.9 all-gather.4
where the time goes:
time: 329 us; the launch traced here: 328 us
  waiting for transfers between devices  237 us (72%)
  blocking collectives  36.2 us (11%)
  matrix products  23.6 us (7%)
  between operations  15.2 us (5%)
  other arithmetic  11.2 us (3%)
  local copies, waits for them, and re-layouts  4.8 us (1%)
    reduce_scatter x2, waiting for transfers between devices, per_device(): lax.psum_scatter(jnp.dot(sig_rows, g_hist, preferred_element_type=jnp.flo...  172 us
    all_gather x2, waiting for transfers between devices, per_device(): lax.all_gather(mine, 'past', axis=0, tiled=True)  65.6 us
    psum x2, blocking collectives, per_device(): total_sq = lax.psum(local_sq, 'second')  36.2 us
    dot_general x2, matrix products, per_device(): jnp.dot(sig_rows, g_hist, preferred_element_type=jnp.float32)  13 us
    dot_general x2, matrix products, per_device(): jnp.dot(w_memory, lax.all_gather(mine, 'past', axis=0, tiled=True), prefe...  7.88 us
  transfers between devices with their start and end apart: 4, of which 4 were waited for; matrix products, arithmetic and copies ran while one was open for 6% of the time, Pallas kernels for 0%

commit v1 on v0

--- a/solution.py
+++ b/solution.py
@@ -28,7 +28,9 @@
         ).astype(jnp.bfloat16)
         gnew = start_value + jnp.dot(
             w_memory,
-            lax.all_gather(mine, "past", axis=0, tiled=True),
+            jnp.concatenate(
+                lax.all_to_all(jnp.stack([mine] * lax.axis_size("past")), "past", 0, 0), axis=0
+            ),
             preferred_element_type=jnp.float32,
         )
         cubic = gnew.reshape(BLK, N, columns) ** 3 * coupling[None]

time: 329 us -> 264 us (0.80)
  waiting for transfers between devices: 237 us -> 165 us
  starting transfers between devices: 0.16 us -> 11.8 us
  other arithmetic: 11.2 us -> 7.52 us
  local copies, waits for them, and re-layouts: 4.8 us -> 8.24 us
    all_gather x2 -> x0, waiting for transfers between devices: 65.6 us -> none  [per_device(): lax.all_gather(mine, 'past', axis=0, tiled=True)]
    all_to_all x0 -> x2, starting transfers between devices: none -> 11.8 us  [per_device(): lax.all_to_all(jnp.stack([mine] * lax.axis_size('past')), 'past', 0, 0)]
    reduce_scatter x2, waiting for transfers between devices: 172 us -> 165 us  [per_device(): lax.psum_scatter(jnp.dot(sig_rows, g_hist, preferred_element_type=jnp.flo...]
  transfers between devices with their start and end apart: 4 -> 4, of which waited for: 4 -> 2; matrix products, arithmetic and copies ran while one was open for 6% -> 7% of each run, Pallas kernels for 0% -> 0%
where the time goes in v1:
time: 264 us; the launch traced here: 263 us
  waiting for transfers between devices  165 us (62%)
  blocking collectives  33.7 us (13%)
  matrix products  21.1 us (8%)
  between operations  15.5 us (6%)
  starting transfers between devices  11.8 us (4%)
  local copies, waits for them, and re-layouts  8.24 us (3%)
  other arithmetic  7.52 us (3%)
    reduce_scatter x2, waiting for transfers between devices, per_device(): lax.psum_scatter(jnp.dot(sig_rows, g_hist, preferred_element_type=jnp.flo...  165 us
    psum x2, blocking collectives, per_device(): total_sq = lax.psum(local_sq, 'second')  33.7 us
    dot_general x2, matrix products, per_device(): jnp.dot(sig_rows, g_hist, preferred_element_type=jnp.float32)  13 us
    all_to_all x2, starting transfers between devices, per_device(): lax.all_to_all(jnp.stack([mine] * lax.axis_size('past')), 'past', 0, 0)  11.8 us
    dot_general x2, matrix products, per_device(): jnp.dot(w_memory, jnp.concatenate(lax.all_to_all(jnp.stack([mine] * lax.a...  5.33 us
  transfers between devices with their start and end apart: 4, of which 2 were waited for; matrix products, arithmetic and copies ran while one was open for 7% of the time, Pallas kernels for 0%

profile of v1, /device:TPU:2, one launch (start us, length us, event | category | flops | bytes accessed | tf_op | source)
XLA Modules:
  0.0 263.4 jit_solution(1361241179617127105)
XLA Ops:
  7.2 0.0 reduce-scatter.3.cloned.1.call-start
  7.2 6.5 %fusion.2 = f32[512,1024]{1,0:T(8,128)} fusion(bf16[2048,1024]{1,0:T(8,128)(2,1)} %param.5, bf16[1024,2048]{1,0:T(8,128)(2,1)} %param.6), kind=kOutput, calls=%fused_computation.14 | convolution fusion | flops 2147483648 | bytes 8388608 | tf_op jit(solution)/shard_map/dot_general | solution.py:24
  13.8 0.0 reduce-scatter.3.cloned.1.call-update
  13.8 0.0 reduce-scatter.5.cloned.1.call-start
  13.8 6.5 %fusion = f32[512,1024]{1,0:T(8,128)} fusion(bf16[2048,1024]{1,0:T(8,128)(2,1)} %param.5, bf16[1024,2048]{1,0:T(8,128)(2,1)} %param.6), kind=kOutput, calls=%fused_computation.10 | convolution fusion | flops 2147483648 | bytes 8388608 | tf_op jit(solution)/shard_map/dot_general | solution.py:24
  20.3 0.0 reduce-scatter.5.cloned.1.call-update
  20.3 82.8 %reduce-scatter.3.cloned.1.call-done = f32[16,1024]{1,0:T(8,128)} async-done(((f32[512,1024]{1,0:T(8,128)}), f32[16,1024]{1,0:T(8,128)}) %reduce-scatter.3.cloned.1.call-update) | async-done | bytes 65552 | tf_op jit(solution)/shard_map/reduce_scatter | solution.py:23
  103.2 0.8 convert_element_type.18
  104.0 1.1 stack.4
  105.1 5.8 %all-to-all-start = ((bf16[32,16,1024]{2,1,0:T(8,128)(2,1)}), bf16[32,16,1024]{2,1,0:T(8,128)(2,1)S(1)}, u32[]{:S(2)}, u32[]{:S(2)}) async-start(bf16[32,16,1024]{2,1,0:T(8,128)(2,1)} %stack.4), calls=%async_computation.1 | async-start | bytes 2097152 | tf_op jit(solution)/shard_map/all_to_all | solution.py:32
  111.0 82.6 %reduce-scatter.5.cloned.1.call-done = f32[16,1024]{1,0:T(8,128)} async-done(((f32[512,1024]{1,0:T(8,128)}), f32[16,1024]{1,0:T(8,128)}) %reduce-scatter.5.cloned.1.call-update) | async-done | bytes 65552 | tf_op jit(solution)/shard_map/reduce_scatter | solution.py:23
  193.6 0.8 convert_element_type.21
  194.4 1.2 stack.5
  195.6 5.9 %all-to-all-start.1 = ((bf16[32,16,1024]{2,1,0:T(8,128)(2,1)}), bf16[32,16,1024]{2,1,0:T(8,128)(2,1)}, u32[]{:S(2)}, u32[]{:S(2)}) async-start(bf16[32,16,1024]{2,1,0:T(8,128)(2,1)} %stack.5), calls=%async_computation.3 | async-start | bytes 2097152 | tf_op jit(solution)/shard_map/all_to_all | solution.py:32
  201.6 2.7 %slice_bitcast_fusion = (bf16[512,1024]{1,0:T(8,128)(2,1)}, bf16[512,1024]{1,0:T(8,128)(2,1)S(1)}) fusion(bf16[2,512,1024]{2,1,0:T(8,128)(2,1)} %param.7), kind=kLoop, calls=%fused_computation.17 | loop fusion | bytes 4194304 | tf_op jit(solution)/shard_map/squeeze | solution.py:21
  204.3 0.7 fusion.8
  205.0 0.2 copy-done.8
  205.2 0.4 copy-done.5
  205.6 1.6 multiply_reduce_fusion.1
  207.1 18.1 %psum.14 = f32[]{:T(128)} all-reduce(f32[]{:T(128)} %get-tuple-element.6), channel_id=1, replica_groups=mesh['past'=32,'second'=8] {'second'}, use_global_device_ids=true, to_apply=%region_2.0 | all-reduce | flops 1 | bytes 8 | tf_op jit(solution)/shard_map/psum | solution.py:38
  225.9 1.4 fusion.10
  227.3 1.0 copy-done.1
  228.2 2.0 fusion.5
  230.3 3.8 %bitcast_convert_fusion = (bf16[512,1024]{1,0:T(8,128)(2,1)}, f32[1024,512]{0,1:T(8,128)S(1)}) fusion(f32[1024,512]{0,1:T(8,128)} %fusion.5, bf16[512,1024]{1,0:T(8,128)(2,1)} %bitcast.5, bf16[512,1024]{1,0:T(8,128)(2,1)} %get-tuple-element.4), kind=kOutput, calls=%fused_computation.6 | convolution fusion | flops 537919488 | bytes 6815744 | tf_op jit(solution)/shard_map/dot_general | solution.py:29
  234.1 1.1 multiply_reduce_fusion
  235.2 15.7 %psum.15 = f32[]{:T(128)} all-reduce(f32[]{:T(128)} %multiply_reduce_fusion), channel_id=1, replica_groups=mesh['past'=32,'second'=8] {'second'}, use_global_device_ids=true, to_apply=%region_5.0 | all-reduce | flops 1 | bytes 8 | tf_op jit(solution)/shard_map/psum | solution.py:38
  251.6 0.3 divide_convert_fusion
  251.9 0.9 copy-done.2
  252.8 1.5 pad_maximum_fusion.1
  254.3 0.0 copy-done.3
  254.3 0.8 copy-done.7
  255.1 1.5 pad_maximum_fusion
  (14 shorter events, 0.0 us)
Async XLA Ops:
  7.2 197.1 %copy-start = (bf16[512,1024]{1,0:T(8,128)(2,1)S(1)}, bf16[512,1024]{1,0:T(8,128)(2,1)}, u32[]{:S(2)}) copy-start(bf16[512,1024]{1,0:T(8,128)(2,1)} %param.8) | copy-start | bytes 3145732
  7.2 96.0 %reduce-scatter.3.cloned.1.call-start = ((), (), s32[]{:S(2)}) async-start(), calls=%async_computation.4 | async-start | bytes 2162688 | tf_op jit(solution)/shard_map/reduce_scatter | solution.py:23
  13.8 179.8 %reduce-scatter.5.cloned.1.call-start = ((), (), s32[]{:S(2)}) async-start(), calls=%async_computation.5 | async-start | bytes 2162688 | tf_op jit(solution)/shard_map/reduce_scatter | solution.py:23
  105.1 89.3 %all-to-all-start = ((bf16[32,16,1024]{2,1,0:T(8,128)(2,1)}), bf16[32,16,1024]{2,1,0:T(8,128)(2,1)S(1)}, u32[]{:S(2)}, u32[]{:S(2)}) async-start(bf16[32,16,1024]{2,1,0:T(8,128)(2,1)} %stack.4), calls=%async_computation.1 | async-start | bytes 2097152 | tf_op jit(solution)/shard_map/all_to_all | solution.py:32
  194.4 9.9 %copy-start.4 = (bf16[32,16,1024]{2,1,0:T(8,128)(2,1)}, bf16[32,16,1024]{2,1,0:T(8,128)(2,1)S(1)}, u32[]{:S(2)}) copy-start(bf16[32,16,1024]{2,1,0:T(8,128)(2,1)S(1)} %all-to-all-done) | copy-start | bytes 3145732
  195.6 34.6 %all-to-all-start.1 = ((bf16[32,16,1024]{2,1,0:T(8,128)(2,1)}), bf16[32,16,1024]{2,1,0:T(8,128)(2,1)}, u32[]{:S(2)}, u32[]{:S(2)}) async-start(bf16[32,16,1024]{2,1,0:T(8,128)(2,1)} %stack.5), calls=%async_computation.3 | async-start | bytes 2097152 | tf_op jit(solution)/shard_map/all_to_all | solution.py:32
  204.3 0.9 copy-start.8
  204.3 1.3 copy-start.5
  225.9 2.4 copy-start.6
  227.3 1.0 copy-start.1
  251.6 1.2 copy-start.2
  252.8 1.5 copy-start.3
  252.8 2.3 copy-start.7
Sparse Core Ops, SparseCore 0:
  13.9 89.2 reduce-scatter.2
  107.6 85.9 reduce-scatter.4
